TPU v7x, 512 devices: a whole 4x4x16 slice. The times are simulated.
512 devices in a mesh: dp: 16 (over z), fsdp: 32 (over x, y, core).
Axes of the slice: x: 4, y: 4, z: 16, core: 2. Of those that a mesh axis runs over, the one named last changes fastest.
Arguments:
- txt_tokens: bfloat16 [512, 8, 3072], P(('dp', 'fsdp')), may hold values from -6 to 6
- concept_table: bfloat16 [4096, 3072], P('dp'), may hold values from -6 to 6
- concept_ids: int32 [512], P(('dp', 'fsdp')), may hold values from 0 to 4095
- positions: int32 [512], P(('dp', 'fsdp')), may hold values from 0 to 7
- timesteps: int32 [512], P(('dp', 'fsdp')), may hold values from 0 to 63
- counts: int32 [4096], P('dp'), may hold values from 1 to 16
- mod_table: bfloat16 [64, 2, 3072], P(None, None, 'fsdp'), may hold values from -1.5 to 1.5
- kv_weight: bfloat16 [3072, 3072], P('fsdp'), may hold values from -0.109375 to 0.109375
- kv_bias: float32 [3072], replicated, may hold values from -3 to 3
- key_gain: float32 [128], replicated, may hold values from 0.5 to 1.5
- img_query: bfloat16 [512, 192, 1536], P(('dp', 'fsdp')), may hold values from -256 to 256
- img_key: bfloat16 [512, 192, 1536], P(('dp', 'fsdp')), may hold values from -6 to 6
- img_value: bfloat16 [512, 192, 1536], P(('dp', 'fsdp')), may hold values from -6 to 6
- out_grad: bfloat16 [512, 192, 1536], P(('dp', 'fsdp')), may hold values from -6 to 6
Outputs:
- table_grad: float32 [4096, 3072], P('dp', 'fsdp')
Inputs may be any that keep to these rules, and one draw needn't show every extreme that they name: `concept_ids`: concept of each sample, some concepts far more common than others.
All inputs are finite; a program needn't handle non-finite values.
Results may differ from a plain program's by a relative error of at most 0.0083.
Values may be sent and summed in bfloat16 or wider, within the bound.
A program may use at most 64 MiB of HBM per device.

v0:
```python
import jax
import jax.numpy as jnp
from jax import lax
from jax.sharding import PartitionSpec as P

EPSILON = 1e-06


def layer_norm(values):
    centre = jnp.mean(values, -1, keepdims=True)
    spread = jnp.mean((values - centre) ** 2, -1, keepdims=True)
    inverse = lax.rsqrt(spread + EPSILON)
    return ((values - centre) * inverse, inverse[..., 0])


def shards(
    txt_tokens,
    concept_table,
    concept_ids,
    positions,
    timesteps,
    counts,
    mod_table,
    kv_weight,
    kv_bias,
    key_gain,
    img_query,
    img_key,
    img_value,
    out_grad,
):
    highest = lax.Precision.HIGHEST
    fsdp_size = lax.axis_size("fsdp")
    column = lax.axis_index("fsdp")
    tok_len = txt_tokens.shape[1]
    model_width = txt_tokens.shape[2]
    slice_width = kv_weight.shape[0]
    kv_width = kv_weight.shape[1]
    head_width = kv_width // 2
    head_dim = key_gain.shape[0]
    head_count = head_width // head_dim
    img_len = img_query.shape[1]
    bucket_count = mod_table.shape[0]
    root_dh = jnp.sqrt(jnp.float32(head_dim))
    table_hat, table_rstd = layer_norm(concept_table.astype(jnp.float32))
    table_part = lax.dynamic_slice_in_dim(
        table_hat.astype(jnp.bfloat16), column * slice_width, slice_width, 1
    )
    table_all = lax.all_gather(table_part, "dp", axis=0, tiled=True)
    own_hat = layer_norm(txt_tokens[0].astype(jnp.float32))[0].astype(jnp.bfloat16)
    labels = jnp.stack([concept_ids[0], positions[0], timesteps[0]])
    label_tile = jnp.tile(labels[None, :], (1, fsdp_size))
    token_cols, label_cols = (
        lax.all_to_all(own_hat, "fsdp", split_axis=1, concat_axis=0, tiled=True),
        lax.all_to_all(label_tile, "fsdp", split_axis=1, concat_axis=0, tiled=True),
    )
    group_ids = label_cols[:, 0]
    group_pos = label_cols[:, 1]
    group_time = label_cols[:, 2]
    concept_cols = jnp.take(table_all, group_ids, axis=0)
    token_cols = token_cols.reshape(fsdp_size, tok_len, slice_width)
    is_place = jnp.arange(tok_len, dtype=jnp.int32)[None, :] == group_pos[:, None]
    token_cols = jnp.where(is_place[:, :, None], concept_cols[:, None, :], token_cols)
    pick_time = (jnp.arange(bucket_count, dtype=jnp.int32)[None, :] == group_time[:, None]).astype(
        jnp.bfloat16
    )
    modulation = jnp.dot(
        pick_time,
        mod_table.reshape(bucket_count, 2 * slice_width),
        preferred_element_type=jnp.float32,
    )
    modulation = modulation.reshape(fsdp_size, 2, slice_width)
    shift_cols = modulation[:, 0]
    scale_cols = 1.0 + modulation[:, 1]
    modulated = (
        scale_cols[:, None, :] * token_cols.astype(jnp.float32) + shift_cols[:, None, :]
    ).astype(jnp.bfloat16)
    kv_terms = jnp.dot(
        modulated.reshape(fsdp_size * tok_len, slice_width),
        kv_weight,
        preferred_element_type=jnp.float32,
    )
    kv_terms = kv_terms.reshape(fsdp_size, tok_len, kv_width)
    weight_f = kv_weight.astype(jnp.float32)
    concept_f = concept_cols.astype(jnp.float32)
    side_rows = jnp.stack([scale_cols, scale_cols * concept_f], 1).reshape(
        fsdp_size * 2, slice_width
    )
    side_terms = jnp.dot(side_rows, weight_f, precision=highest).reshape(fsdp_size, 2, kv_width)
    all_terms = jnp.concatenate([kv_terms, side_terms], 1)
    row_block = all_terms.shape[1]
    all_terms = all_terms.reshape(fsdp_size * row_block, kv_width)
    own_rows = lax.psum_scatter(all_terms, "fsdp", scatter_dimension=0, tiled=True)
    kv_rows = own_rows[:tok_len] + kv_bias
    pos_pick = (jnp.arange(tok_len, dtype=jnp.int32) == positions[0]).astype(jnp.float32)
    key_raw = kv_rows[:, :head_width].reshape(tok_len, head_count, head_dim)
    key_inv = lax.rsqrt(jnp.mean(key_raw * key_raw, -1) + EPSILON)
    key_norm = (
        (key_raw * key_inv[..., None] * key_gain).astype(jnp.bfloat16).reshape(tok_len, head_width)
    )
    val_txt = kv_rows[:, head_width:].astype(jnp.bfloat16)
    keys_all = jnp.concatenate([key_norm, img_key[0]], 0).reshape(
        tok_len + img_len, head_count, head_dim
    )
    vals_all = jnp.concatenate([val_txt, img_value[0]], 0).reshape(
        tok_len + img_len, head_count, head_dim
    )
    queries = img_query[0].reshape(img_len, head_count, head_dim)
    scores = (
        jnp.einsum("qhd,khd->hqk", queries, keys_all, preferred_element_type=jnp.float32) / root_dh
    )
    row_top = jnp.max(scores, -1, keepdims=True)
    raised = jnp.exp(scores - row_top)
    prob_full = raised / jnp.sum(raised, -1, keepdims=True)
    prob_low = prob_full.astype(jnp.bfloat16)
    attended = jnp.einsum("hqk,khd->qhd", prob_low, vals_all, preferred_element_type=jnp.float32)
    grad_f = out_grad[0].reshape(img_len, head_count, head_dim).astype(jnp.float32)
    row_delta = jnp.einsum("qhd,qhd->hq", grad_f, attended)
    prob_pos = jnp.einsum("hqk,k->hq", prob_full[:, :, :tok_len], pos_pick, precision=highest)
    val_local = val_txt.reshape(tok_len, head_count, head_dim).astype(jnp.float32)
    val_pos = jnp.einsum("k,khd->hd", pos_pick, val_local, precision=highest)
    grad_prob = jnp.einsum("qhd,hd->hq", grad_f, val_pos, precision=highest)
    grad_score = prob_pos * (grad_prob - row_delta)
    grad_val = jnp.einsum("hq,qhd->hd", prob_pos, grad_f, precision=highest)
    grad_key = (
        jnp.einsum("hq,qhd->hd", grad_score, queries.astype(jnp.float32), precision=highest)
        / root_dh
    )
    raw_pos = jnp.einsum("k,khd->hd", pos_pick, key_raw, precision=highest)
    inv_pos = jnp.einsum("k,kh->h", pos_pick, key_inv, precision=highest)
    normed_key = raw_pos * inv_pos[:, None]
    grad_norm = grad_key * key_gain
    grad_raw = inv_pos[:, None] * (
        grad_norm - normed_key * jnp.mean(grad_norm * normed_key, -1, keepdims=True)
    )
    grad_kv = jnp.concatenate([grad_raw.reshape(head_width), grad_val.reshape(head_width)])[None, :]
    side_mean = (
        jnp.stack(
            [
                jnp.dot(grad_kv[0], own_rows[tok_len], precision=highest),
                jnp.dot(grad_kv[0], own_rows[tok_len + 1], precision=highest),
            ]
        )
        / model_width
    )
    grads_all, sides_all = (
        lax.all_gather(grad_kv, "fsdp", axis=0, tiled=True),
        lax.all_gather(side_mean[None, :], "fsdp", axis=0, tiled=True),
    )
    grad_cols = jnp.dot(grads_all, weight_f.T, precision=highest) * scale_cols
    row_grad = grad_cols - sides_all[:, 0:1] - concept_f * sides_all[:, 1:2]
    owner_scale = table_rstd / counts.astype(jnp.float32)
    conc_total = table_all.shape[0]
    one_hot = (jnp.arange(conc_total, dtype=jnp.int32)[:, None] == group_ids[None, :]).astype(
        jnp.float32
    )
    dense_rows = jnp.dot(one_hot, row_grad, precision=highest)
    owned_rows = lax.psum_scatter(dense_rows, "dp", scatter_dimension=0, tiled=True)
    return owned_rows * owner_scale[:, None]


def solution(mesh):
    placed = (
        P(("dp", "fsdp"), None, None),
        P("dp", None),
        P(("dp", "fsdp")),
        P(("dp", "fsdp")),
        P(("dp", "fsdp")),
        P("dp"),
        P(None, None, "fsdp"),
        P("fsdp", None),
        P(),
        P(),
        P(("dp", "fsdp"), None, None),
        P(("dp", "fsdp"), None, None),
        P(("dp", "fsdp"), None, None),
        P(("dp", "fsdp"), None, None),
    )
    return jax.shard_map(
        shards, mesh=mesh, in_specs=placed, out_specs=P("dp", "fsdp"), check_vma=False
    )
```

profile of v0, /device:TPU:2, one launch (start us, length us, event | category | flops | bytes accessed | tf_op | source)
XLA Modules:
  0.0 369.3 jit_solution(15416597220606547347)
XLA Ops:
  9.3 9.3 %all-to-all-start = ((s32[1,32,3]{2,0,1:T(1,128)}), s32[1,32,3]{2,0,1:T(1,128)S(1)}, u32[]{:S(2)}, u32[]{:S(2)}) async-start(s32[1,32,3]{2,0,1:T(1,128)} %tile.2), calls=%async_computation | async-start | bytes 32768 | tf_op jit(solution)/shard_map/all_to_all | solution.py:55
  20.5 1.7 convert_reduce_fusion
  22.3 2.1 multiply_reduce_fusion
  25.0 1.1 fusion.32
  26.1 39.8 %all_gather.9 = bf16[4096,96]{1,0:T(8,128)(2,1)S(1)} all-gather(bf16[256,96]{1,0:T(8,128)(2,1)S(1)} %fusion.32), channel_id=1, replica_groups=mesh['dp'=16,'fsdp'=32] {'dp'}, dimensions={0}, use_global_device_ids=true | all-gather | bytes 835584 | tf_op jit(solution)/shard_map/all_gather | solution.py:49
  67.1 7.4 %all-to-all-start.1 = ((bf16[8,32,96]{2,0,1:T(8,128)(2,1)}), bf16[8,32,96]{2,0,1:T(8,128)(2,1)S(1)}, u32[]{:S(2)}, u32[]{:S(2)}) async-start(bf16[8,32,96]{2,0,1:T(8,128)(2,1)} %fusion.34), calls=%async_computation.1 | async-start | bytes 131072 | tf_op jit(solution)/shard_map/all_to_all | solution.py:54
  77.8 3.0 all-to-all-done.1
  81.4 3.4 pad_maximum_fusion
  84.8 5.3 %reshape.229 = f32[320,3072]{1,0:T(8,128)} reshape(f32[32,10,3072]{2,1,0:T(8,128)} %pad_maximum_fusion) | data formatting | bytes 7864320 | tf_op jit(solution)/shard_map/reshape | solution.py:92
  90.2 1.0 copy-done.7
  92.8 2.2 reshape_squeeze.7
  95.0 1.3 dynamic-slice
  97.4 126.6 %all-reduce.3.cloned.1.call-done = f32[320,3072]{1,0:T(8,128)} async-done(((f32[320,3072]{1,0:T(8,128)}), f32[320,3072]{1,0:T(8,128)}) %all-reduce.3.cloned.1.call-update) | async-done | bytes 3932176
  225.7 2.5 fusion.79
  230.7 1.0 fusion.6
  231.9 2.1 fusion.26
  234.0 1.7 fusion.28
  236.9 1.0 constant_dynamic-slice_fusion.1
  238.6 1.4 fusion.68
  240.0 20.8 %all-gather.1 = f32[32,1,2]{2,1,0:T(1,128)S(1)} all-gather(f32[1,1,2]{2,1,0:T(1,128)S(1)} %fusion.68), channel_id=1, replica_groups=mesh['dp'=16,'fsdp'=32] {'fsdp'}, dimensions={0}, use_global_device_ids=true | all-gather | bytes 264 | tf_op jit(solution)/shard_map/all_gather | solution.py:148
  260.9 24.3 %all-gather = f32[98304]{0:T(1024)S(1)} all-gather(f32[3072]{0:T(1024)S(1)} %get-tuple-element.7), channel_id=2, replica_groups=mesh['dp'=16,'fsdp'=32] {'fsdp'}, dimensions={0}, use_global_device_ids=true | all-gather | bytes 405504 | tf_op jit(solution)/shard_map/all_gather | solution.py:147
  285.9 2.0 fusion.23
  287.9 73.0 %reduce-scatter.2.cloned.1.call-done = f32[256,96]{0,1:T(8,128)} async-done(((f32[4096,96]{0,1:T(8,128)}), f32[256,96]{0,1:T(8,128)}) %reduce-scatter.2.cloned.1.call-update) | async-done | bytes 98320 | tf_op jit(solution)/shard_map/reduce_scatter | solution.py:158
  360.9 1.5 broadcast_multiply_fusion
  (100 shorter events, 17.2 us)
Async XLA Ops:
  6.5 70.1 %copy-start = (bf16[96,3072]{1,0:T(8,128)(2,1)S(1)}, bf16[96,3072]{1,0:T(8,128)(2,1)}, u32[]{:S(2)}) copy-start(bf16[96,3072]{1,0:T(8,128)(2,1)} %param.21) | copy-start | bytes 1769476
  6.5 15.7 %copy-start.1 = (bf16[256,3072]{1,0:T(8,128)(2,1)S(1)}, bf16[256,3072]{1,0:T(8,128)(2,1)}, u32[]{:S(2)}) copy-start(bf16[256,3072]{1,0:T(8,128)(2,1)} %param.15) | copy-start | bytes 4718596
  9.3 57.8 %all-to-all-start = ((s32[1,32,3]{2,0,1:T(1,128)}), s32[1,32,3]{2,0,1:T(1,128)S(1)}, u32[]{:S(2)}, u32[]{:S(2)}) async-start(s32[1,32,3]{2,0,1:T(1,128)} %tile.2), calls=%async_computation | async-start | bytes 32768 | tf_op jit(solution)/shard_map/all_to_all | solution.py:55
  22.2 2.2 copy-start.18
  22.2 43.7 %copy-start.10 = (bf16[1,8,3072]{2,1,0:T(8,128)(2,1)S(1)}, bf16[1,8,3072]{2,1,0:T(8,128)(2,1)}, u32[]{:S(2)}) copy-start(bf16[1,8,3072]{2,1,0:T(8,128)(2,1)} %param.14) | copy-start | bytes 147460
  22.3 44.6 %copy-start.13 = (bf16[64,2,96]{2,1,0:T(2,128)(2,1)S(1)}, bf16[64,2,96]{2,1,0:T(2,128)(2,1)}, u32[]{:S(2)}) copy-start(bf16[64,2,96]{2,1,0:T(2,128)(2,1)} %param.20) | copy-start | bytes 73732
  67.1 13.7 %all-to-all-start.1 = ((bf16[8,32,96]{2,0,1:T(8,128)(2,1)}), bf16[8,32,96]{2,0,1:T(8,128)(2,1)S(1)}, u32[]{:S(2)}, u32[]{:S(2)}) async-start(bf16[8,32,96]{2,0,1:T(8,128)(2,1)} %fusion.34), calls=%async_computation.1 | async-start | bytes 131072 | tf_op jit(solution)/shard_map/all_to_all | solution.py:54
  74.5 149.5 %all-reduce.3.cloned.1.call-start = ((), (), s32[]{:S(2)}) async-start(), calls=%async_computation.4 | async-start | bytes 7864320
  76.0 0.6 copy-start.11
  90.1 1.1 copy-start.7
  90.1 1.5 copy-start.8
  90.1 2.1 copy-start.9
  90.1 270.8 %reduce-scatter.2.cloned.1.call-start = ((), (), s32[]{:S(2)}) async-start(), calls=%async_computation.3 | async-start | bytes 1671168 | tf_op jit(solution)/shard_map/reduce_scatter | solution.py:158
  91.6 133.6 %copy-start.4 = (bf16[192,12,128]{2,1,0:T(8,128)(2,1)}, bf16[192,12,128]{2,1,0:T(8,128)(2,1)S(1)}, u32[]{:S(2)}) copy-start(bf16[192,12,128]{2,1,0:T(8,128)(2,1)S(1)} %reshape_squeeze.6) | copy-start | bytes 1769476
  92.2 4.8 %copy-start.19 = (f32[128]{0:T(128)S(1)}, f32[128]{0:T(128)}, u32[]{:S(2)}) copy-start(f32[128]{0:T(128)} %param.23) | copy-start | bytes 1540
  92.6 131.4 %copy-start.14 = (f32[3072]{0:T(1024)S(1)}, f32[3072]{0:T(1024)}, u32[]{:S(2)}) copy-start(f32[3072]{0:T(1024)} %param.22) | copy-start | bytes 36868
  225.0 3.2 copy-start.5
  228.6 1.1 copy-start.2
  229.7 2.0 copy-start.6
  229.8 6.3 %copy-start.17 = (f32[128]{0:T(128)S(1)}, f32[128]{0:T(128)}, u32[]{:S(2)}) copy-start(f32[128]{0:T(128)} %broadcast_multiply_fusion.3) | copy-start | bytes 1540
  230.7 5.7 %copy-start.3 = (bf16[192,12,128]{2,1,0:T(8,128)(2,1)S(1)}, bf16[192,12,128]{2,1,0:T(8,128)(2,1)}, u32[]{:S(2)}) copy-start(bf16[192,12,128]{2,1,0:T(8,128)(2,1)} %reshape_squeeze.7) | copy-start | bytes 1769476
  230.7 54.6 %copy-start.12 = (f32[32,2,96]{2,0,1:T(8,128)S(1)}, f32[32,2,96]{2,0,1:T(8,128)}, u32[]{:S(2)}) copy-start(f32[32,2,96]{2,0,1:T(8,128)} %copy-done.11) | copy-start | bytes 73732
  231.7 54.2 %copy-start.16 = (s32[32]{0:T(128)S(1)}, s32[32]{0:T(128)}, u32[]{:S(2)}) copy-start(s32[32]{0:T(128)} %get-tuple-element.16) | copy-start | bytes 388
  285.2 75.7 %copy-start.15 = (f32[256]{0:T(256)S(1)}, f32[256]{0:T(256)}, u32[]{:S(2)}) copy-start(f32[256]{0:T(256)} %get-tuple-element.20) | copy-start | bytes 3076
Sparse Core Ops, SparseCore 0:
  90.2 133.7 all-reduce.2
  288.1 72.8 reduce-scatter.1
where the time goes:
time: 370 us; the launch traced here: 369 us
  waiting for transfers between devices  203 us (55%)
  blocking collectives  84.9 us (23%)
  other arithmetic  21 us (6%)
  starting transfers between devices  16.8 us (5%)
  local copies, waits for them, and re-layouts  16.7 us (5%)
  between operations  16.5 us (4%)
  matrix products  10.8 us (3%)
    unnamed x3, waiting for transfers between devices  127 us
    reduce_scatter x1, waiting for transfers between devices, shards(): lax.psum_scatter(dense_rows, 'dp', scatter_dimension=0, tiled=True)  73 us
    all_gather x1, blocking collectives, shards(): table_all = lax.all_gather(table_part, 'dp', axis=0, tiled=True)  39.8 us
    all_gather x1, blocking collectives, shards(): lax.all_gather(grad_kv, 'fsdp', axis=0, tiled=True)  24.3 us
    all_gather x1, blocking collectives, shards(): lax.all_gather(side_mean[None, :], 'fsdp', axis=0, tiled=True)  20.8 us
    all_to_all x1, starting transfers between devices, shards(): lax.all_to_all(label_tile, 'fsdp', split_axis=1, concat_axis=0, tiled=True)  9.32 us
  transfers between devices with their start and end apart: 4, of which 3 were waited for; matrix products, arithmetic and copies ran while one was open for 5% of the time, Pallas kernels for 0%

commit v1 on v0

--- a/solution.py
+++ b/solution.py
@@ -4,6 +4,11 @@
 from jax.sharding import PartitionSpec as P
 
 EPSILON = 1e-06
+
+
+def gather_from_all(array, axis, dim):
+    copies = jnp.concatenate([array] * lax.axis_size(axis), axis=dim)
+    return lax.all_to_all(copies, axis, dim, dim, tiled=True)
 
 
 def layer_norm(values):
@@ -144,7 +149,7 @@
         / model_width
     )
     grads_all, sides_all = (
-        lax.all_gather(grad_kv, "fsdp", axis=0, tiled=True),
+        gather_from_all(grad_kv, "fsdp", 0),
         lax.all_gather(side_mean[None, :], "fsdp", axis=0, tiled=True),
     )
     grad_cols = jnp.dot(grads_all, weight_f.T, precision=highest) * scale_cols

time: 370 us -> 354 us (0.957)
  blocking collectives: 84.9 us -> 61.2 us
  starting transfers between devices: 16.8 us -> 23.6 us
    all_gather x1 -> x0, blocking collectives: 24.3 us -> none  [shards(): lax.all_gather(grad_kv, 'fsdp', axis=0, tiled=True)]
    all_to_all x0 -> x1, starting transfers between devices: none -> 6.62 us  [gather_from_all(): return lax.all_to_all(copies, axis, dim, dim, tiled=True)]
  transfers between devices with their start and end apart: 4 -> 5, of which waited for: 3 -> 3; matrix products, arithmetic and copies ran while one was open for 5% -> 5% of each run, Pallas kernels for 0% -> 0%
where the time goes in v1:
time: 354 us; the launch traced here: 353 us
  waiting for transfers between devices  202 us (57%)
  blocking collectives  61.2 us (17%)
  starting transfers between devices  23.6 us (7%)
  other arithmetic  20.9 us (6%)
  local copies, waits for them, and re-layouts  17.6 us (5%)
  between operations  16.5 us (5%)
  matrix products  10.7 us (3%)
    unnamed x3, waiting for transfers between devices  127 us
    reduce_scatter x1, waiting for transfers between devices, shards(): lax.psum_scatter(dense_rows, 'dp', scatter_dimension=0, tiled=True)  72.8 us
    all_gather x1, blocking collectives, shards(): table_all = lax.all_gather(table_part, 'dp', axis=0, tiled=True)  39.8 us
    all_gather x1, blocking collectives, shards(): lax.all_gather(side_mean[None, :], 'fsdp', axis=0, tiled=True)  21.3 us
    all_to_all x1, starting transfers between devices, shards(): lax.all_to_all(label_tile, 'fsdp', split_axis=1, concat_axis=0, tiled=True)  9.32 us
    all_to_all x1, starting transfers between devices, shards(): lax.all_to_all(own_hat, 'fsdp', split_axis=1, concat_axis=0, tiled=True)  7.39 us
  transfers between devices with their start and end apart: 5, of which 3 were waited for; matrix products, arithmetic and copies ran while one was open for 5% of the time, Pallas kernels for 0%

profile of v1, /device:TPU:2, one launch (start us, length us, event | category | flops | bytes accessed | tf_op | source)
XLA Modules:
  0.0 352.8 jit_solution(4657196009542717818)
XLA Ops:
  9.3 9.3 %all-to-all-start = ((s32[1,32,3]{2,0,1:T(1,128)}), s32[1,32,3]{2,0,1:T(1,128)S(1)}, u32[]{:S(2)}, u32[]{:S(2)}) async-start(s32[1,32,3]{2,0,1:T(1,128)} %tile.2), calls=%async_computation | async-start | bytes 32768 | tf_op jit(solution)/shard_map/all_to_all | solution.py:60
  20.5 1.7 convert_reduce_fusion
  22.3 2.1 multiply_reduce_fusion
  25.0 1.1 fusion.34
  26.1 39.8 %all_gather.6 = bf16[4096,96]{1,0:T(8,128)(2,1)S(1)} all-gather(bf16[256,96]{1,0:T(8,128)(2,1)S(1)} %fusion.34), channel_id=1, replica_groups=mesh['dp'=16,'fsdp'=32] {'dp'}, dimensions={0}, use_global_device_ids=true | all-gather | bytes 835584 | tf_op jit(solution)/shard_map/all_gather | solution.py:54
  67.1 7.4 %all-to-all-start.1 = ((bf16[8,32,96]{2,0,1:T(8,128)(2,1)}), bf16[8,32,96]{2,0,1:T(8,128)(2,1)S(1)}, u32[]{:S(2)}, u32[]{:S(2)}) async-start(bf16[8,32,96]{2,0,1:T(8,128)(2,1)} %fusion.36), calls=%async_computation.1 | async-start | bytes 131072 | tf_op jit(solution)/shard_map/all_to_all | solution.py:59
  78.0 2.9 all-to-all-done.1
  81.4 3.4 pad_maximum_fusion
  84.8 5.3 %reshape.236 = f32[320,3072]{1,0:T(8,128)} reshape(f32[32,10,3072]{2,1,0:T(8,128)} %pad_maximum_fusion) | data formatting | bytes 7864320 | tf_op jit(solution)/shard_map/reshape | solution.py:97
  90.1 1.0 copy-done.7
  92.8 2.2 reshape_squeeze.7
  95.0 1.3 dynamic-slice
  97.4 126.6 %all-reduce.3.cloned.1.call-done = f32[320,3072]{1,0:T(8,128)} async-done(((f32[320,3072]{1,0:T(8,128)}), f32[320,3072]{1,0:T(8,128)}) %all-reduce.3.cloned.1.call-update) | async-done | bytes 3932176
  225.7 2.5 fusion.81
  230.7 1.0 fusion.6
  231.9 2.1 fusion.26
  234.0 1.7 fusion.28
  236.9 1.0 constant_dynamic-slice_fusion.1
  239.5 6.6 %all-to-all-start.2 = ((f32[32,1,3072]{2,1,0:T(1,128)}), f32[32,1,3072]{2,1,0:T(1,128)S(1)}, u32[]{:S(2)}, u32[]{:S(2)}) async-start(f32[32,1,3072]{2,1,0:T(1,128)} %concatenate.37), calls=%async_computation.2 | async-start | bytes 786432 | tf_op jit(solution)/shard_map/all_to_all | solution.py:11
  246.2 1.3 fusion.70
  247.6 21.3 %all-gather = f32[32,1,2]{2,1,0:T(1,128)S(1)} all-gather(f32[1,1,2]{2,1,0:T(1,128)S(1)} %fusion.70), channel_id=1, replica_groups=mesh['dp'=16,'fsdp'=32] {'fsdp'}, dimensions={0}, use_global_device_ids=true | all-gather | bytes 264 | tf_op jit(solution)/shard_map/all_gather | solution.py:153
  269.6 2.0 fusion.23
  271.6 72.8 %reduce-scatter.2.cloned.1.call-done = f32[256,96]{0,1:T(8,128)} async-done(((f32[4096,96]{0,1:T(8,128)}), f32[256,96]{0,1:T(8,128)}) %reduce-scatter.2.cloned.1.call-update) | async-done | bytes 98320 | tf_op jit(solution)/shard_map/reduce_scatter | solution.py:163
  344.4 1.5 broadcast_multiply_fusion
  (101 shorter events, 18.2 us)
Async XLA Ops:
  6.5 70.3 %copy-start = (bf16[96,3072]{1,0:T(8,128)(2,1)S(1)}, bf16[96,3072]{1,0:T(8,128)(2,1)}, u32[]{:S(2)}) copy-start(bf16[96,3072]{1,0:T(8,128)(2,1)} %param.21) | copy-start | bytes 1769476
  6.5 15.7 %copy-start.1 = (bf16[256,3072]{1,0:T(8,128)(2,1)S(1)}, bf16[256,3072]{1,0:T(8,128)(2,1)}, u32[]{:S(2)}) copy-start(bf16[256,3072]{1,0:T(8,128)(2,1)} %param.15) | copy-start | bytes 4718596
  9.3 57.8 %all-to-all-start = ((s32[1,32,3]{2,0,1:T(1,128)}), s32[1,32,3]{2,0,1:T(1,128)S(1)}, u32[]{:S(2)}, u32[]{:S(2)}) async-start(s32[1,32,3]{2,0,1:T(1,128)} %tile.2), calls=%async_computation | async-start | bytes 32768 | tf_op jit(solution)/shard_map/all_to_all | solution.py:60
  22.2 2.2 copy-start.18
  22.2 43.7 %copy-start.10 = (bf16[1,8,3072]{2,1,0:T(8,128)(2,1)S(1)}, bf16[1,8,3072]{2,1,0:T(8,128)(2,1)}, u32[]{:S(2)}) copy-start(bf16[1,8,3072]{2,1,0:T(8,128)(2,1)} %param.14) | copy-start | bytes 147460
  22.3 44.6 %copy-start.13 = (bf16[64,2,96]{2,1,0:T(2,128)(2,1)S(1)}, bf16[64,2,96]{2,1,0:T(2,128)(2,1)}, u32[]{:S(2)}) copy-start(bf16[64,2,96]{2,1,0:T(2,128)(2,1)} %param.20) | copy-start | bytes 73732
  67.1 13.7 %all-to-all-start.1 = ((bf16[8,32,96]{2,0,1:T(8,128)(2,1)}), bf16[8,32,96]{2,0,1:T(8,128)(2,1)S(1)}, u32[]{:S(2)}, u32[]{:S(2)}) async-start(bf16[8,32,96]{2,0,1:T(8,128)(2,1)} %fusion.36), calls=%async_computation.1 | async-start | bytes 131072 | tf_op jit(solution)/shard_map/all_to_all | solution.py:59
  74.5 149.5 %all-reduce.3.cloned.1.call-start = ((), (), s32[]{:S(2)}) async-start(), calls=%async_computation.5 | async-start | bytes 7864320
  90.1 1.1 copy-start.7
  90.1 1.5 copy-start.8
  90.1 2.1 copy-start.9
  91.6 133.6 %copy-start.4 = (bf16[192,12,128]{2,1,0:T(8,128)(2,1)}, bf16[192,12,128]{2,1,0:T(8,128)(2,1)S(1)}, u32[]{:S(2)}) copy-start(bf16[192,12,128]{2,1,0:T(8,128)(2,1)S(1)} %reshape_squeeze.6) | copy-start | bytes 1769476
  92.2 4.8 %copy-start.19 = (f32[128]{0:T(128)S(1)}, f32[128]{0:T(128)}, u32[]{:S(2)}) copy-start(f32[128]{0:T(128)} %param.23) | copy-start | bytes 1540
  92.6 131.4 %copy-start.14 = (f32[3072]{0:T(1024)S(1)}, f32[3072]{0:T(1024)}, u32[]{:S(2)}) copy-start(f32[3072]{0:T(1024)} %param.22) | copy-start | bytes 36868
  225.0 3.2 copy-start.5
  228.6 1.1 copy-start.2
  229.7 2.0 copy-start.6
  229.8 6.3 %copy-start.17 = (f32[128]{0:T(128)S(1)}, f32[128]{0:T(128)}, u32[]{:S(2)}) copy-start(f32[128]{0:T(128)} %broadcast_multiply_fusion.3) | copy-start | bytes 1540
  230.7 5.7 %copy-start.3 = (bf16[192,12,128]{2,1,0:T(8,128)(2,1)S(1)}, bf16[192,12,128]{2,1,0:T(8,128)(2,1)}, u32[]{:S(2)}) copy-start(bf16[192,12,128]{2,1,0:T(8,128)(2,1)} %reshape_squeeze.7) | copy-start | bytes 1769476
  230.7 38.3 %copy-start.12 = (f32[32,2,96]{2,0,1:T(8,128)S(1)}, f32[32,2,96]{2,0,1:T(8,128)}, u32[]{:S(2)}) copy-start(f32[32,2,96]{2,0,1:T(8,128)} %copy-done.11) | copy-start | bytes 73732
  231.7 37.9 %copy-start.16 = (s32[32]{0:T(128)S(1)}, s32[32]{0:T(128)}, u32[]{:S(2)}) copy-start(s32[32]{0:T(128)} %get-tuple-element.16) | copy-start | bytes 388
  239.5 104.9 %copy-start.15 = (f32[256]{0:T(256)S(1)}, f32[256]{0:T(256)}, u32[]{:S(2)}) copy-start(f32[256]{0:T(256)} %get-tuple-element.20) | copy-start | bytes 3076
  239.5 29.4 %all-to-all-start.2 = ((f32[32,1,3072]{2,1,0:T(1,128)}), f32[32,1,3072]{2,1,0:T(1,128)S(1)}, u32[]{:S(2)}, u32[]{:S(2)}) async-start(f32[32,1,3072]{2,1,0:T(1,128)} %concatenate.37), calls=%async_computation.2 | async-start | bytes 786432 | tf_op jit(solution)/shard_map/all_to_all | solution.py:11
  246.2 98.2 %reduce-scatter.2.cloned.1.call-start = ((), (), s32[]{:S(2)}) async-start(), calls=%async_computation.4 | async-start | bytes 1671168 | tf_op jit(solution)/shard_map/reduce_scatter | solution.py:163
  (1 other events, 0.6 us)
Sparse Core Ops, SparseCore 0:
  90.2 133.7 all-reduce.2
  271.7 72.6 reduce-scatter.1
